TPU v7x, 32 devices: a whole 2x2x4 slice. The times are simulated.
32 devices in a mesh: ctx: 4 (over z), section: 2 (over x), mp: 4 (over y, core).
Axes of the slice: x: 2, y: 2, z: 4, core: 2. Of those that a mesh axis runs over, the one named last changes fastest.
Arguments:
- patches: bfloat16 [2, 768, 3200], P(None, ('ctx', 'mp')), may hold values from -16 to 16
- carried: bfloat16 [768, 3200], P(('ctx', 'mp')), may hold values from -16 to 16
- norm_gain: float32 [2, 3200], P('section'), may hold values from 0.1 to 1.9
- q_gain: float32 [2, 128], P('section'), may hold values from 1.5 to 2.5
- k_gain: float32 [2, 128], P('section'), may hold values from 1.5 to 2.5
- q_weight: bfloat16 [2, 3200, 2048], P('section', None, 'mp'), may hold values from -0.109375 to 0.109375
- k_weight: bfloat16 [2, 3200, 2048], P('section', None, 'mp'), may hold values from -0.109375 to 0.109375
- v_weight: bfloat16 [2, 3200, 2048], P('section', None, 'mp'), may hold values from -0.109375 to 0.109375
- o_weight: bfloat16 [2, 2048, 3200], P('section', 'mp', 'ctx'), may hold values from -0.125 to 0.125
Outputs:
- section_outputs: bfloat16 [2, 2, 768, 3200], P('section', None, ('ctx', 'mp'))
All inputs are finite; a program needn't handle non-finite values.
Results may differ from a plain program's by a relative error of at most 0.0063.
Values may be sent and summed in bfloat16 or wider, within the bound.
A program may use at most 128 MiB of HBM per device.

v0:
```python
import math
import jax
import jax.numpy as jnp
from jax import lax
from jax.sharding import PartitionSpec as P

epsilon = 1e-06


def shifted(value, axis, steps):
    count = lax.axis_size(axis)
    leading, last = (max(0, -steps), min(count, count - steps))
    return lax.ppermute(value, axis, [(source, source + steps) for source in range(leading, last)])


def rms_scaled(values, gain):
    return values * lax.rsqrt(jnp.mean(values * values, axis=-1, keepdims=True) + epsilon) * gain


def per_device(patches, carried, norm_gain, q_gain, k_gain, q_weight, k_weight, v_weight, o_weight):
    micro_count = patches.shape[0]
    head_dim = q_gain.shape[1]
    head_count = q_weight.shape[2] // head_dim
    columns = head_count * head_dim
    score_scale = 1.0 / math.sqrt(head_dim)
    section_index = lax.axis_index("section")
    layer_gain = norm_gain[0]
    query_gain = q_gain[0]
    key_gain = k_gain[0]
    incoming = carried
    results = []
    for micro_step in range(micro_count):
        layer_input = jnp.where(section_index == 0, patches[micro_step], incoming)
        residual = layer_input.astype(jnp.float32)
        normed = rms_scaled(residual, layer_gain).astype(jnp.bfloat16)
        project_segment = lax.all_gather(normed, "mp", axis=0, tiled=True)
        project_count = project_segment.shape[0]
        raw_query = jnp.dot(project_segment, q_weight[0], preferred_element_type=jnp.float32)
        raw_key = jnp.dot(project_segment, k_weight[0], preferred_element_type=jnp.float32)
        raw_value = jnp.dot(project_segment, v_weight[0], preferred_element_type=jnp.float32)
        query_rows = rms_scaled(
            raw_query.reshape(project_count, head_count, head_dim), query_gain
        ).reshape(project_count, columns)
        key_rows = rms_scaled(
            raw_key.reshape(project_count, head_count, head_dim), key_gain
        ).reshape(project_count, columns)
        projected = jnp.stack(
            (
                query_rows.astype(jnp.bfloat16),
                key_rows.astype(jnp.bfloat16),
                raw_value.astype(jnp.bfloat16),
            ),
            0,
        )
        block_count = projected.shape[1]
        attend_queries = projected[0].reshape(block_count, head_count, head_dim)
        key_block = lax.all_gather(projected[1], "ctx", axis=0, tiled=True)
        count = key_block.shape[0]
        scores = (
            jnp.einsum(
                "qhd,khd->qhk",
                attend_queries,
                key_block.reshape(count, head_count, head_dim),
                preferred_element_type=jnp.float32,
            )
            * score_scale
        )
        probs = jnp.exp(scores)
        totals = jnp.sum(probs, axis=2)
        weighted = jnp.einsum(
            "qhk,khd->qhd",
            probs.astype(jnp.bfloat16),
            lax.all_gather(projected[2], "ctx", axis=0, tiled=True).reshape(
                count, head_count, head_dim
            ),
            preferred_element_type=jnp.float32,
        )
        attended = (
            (weighted / totals[:, :, None]).reshape(block_count, columns).astype(jnp.bfloat16)
        )
        partial_value = jnp.dot(
            attended,
            lax.all_gather(o_weight[0], "ctx", axis=1, tiled=True),
            preferred_element_type=jnp.float32,
        )
        summed = lax.psum_scatter(partial_value, "mp", scatter_dimension=0, tiled=True)
        layer_out = (residual + summed).astype(jnp.bfloat16)
        results.append(layer_out)
        if micro_step + 1 < micro_count:
            incoming = shifted(layer_out, "section", 1)
    return jnp.stack(results)[None]


def solution(mesh):
    in_specs = (
        P(None, ("ctx", "mp"), None),
        P(("ctx", "mp"), None),
        P("section", None),
        P("section", None),
        P("section", None),
        P("section", None, "mp"),
        P("section", None, "mp"),
        P("section", None, "mp"),
        P("section", "mp", "ctx"),
    )
    out_specs = P("section", None, ("ctx", "mp"), None)
    return jax.shard_map(
        per_device, mesh=mesh, in_specs=in_specs, out_specs=out_specs, check_vma=False
    )
```

profile of v0, /device:TPU:0, one launch (start us, length us, event | category | flops | bytes accessed | tf_op | source)
XLA Modules:
  0.0 286.1 jit_solution(7352324095041157773)
XLA Ops:
  6.5 2.0 fusion.34
  9.4 1.8 fusion.36
  12.0 5.6 %copy.32 = bf16[512,3200]{1,0:T(8,128)(2,1)} copy(bf16[512,3200]{0,1:T(8,128)(2,1)} %bitcast.129) | data formatting | bytes 6553600 | tf_op jit(solution)/shard_map/dot_general | solution.py:39
  17.6 5.8 %copy.33 = bf16[512,3200]{1,0:T(8,128)(2,1)} copy(bf16[512,3200]{0,1:T(8,128)(2,1)} %bitcast.130) | data formatting | bytes 6553600 | tf_op jit(solution)/shard_map/dot_general | solution.py:38
  23.5 8.4 %all-gather.5.cloned.1.call-done = bf16[192,3200]{1,0:T(8,128)(2,1)} async-done(((bf16[48,3200]{1,0:T(8,128)(2,1)}), bf16[192,3200]{1,0:T(8,128)(2,1)}) %all-gather.5.cloned.1.call-update) | async-done | bytes 1228816 | tf_op jit(solution)/shard_map/all_gather | solution.py:36
  31.9 3.7 %multiply_reduce_fusion.3 = (f32[192,4]{0,1:T(4,128)S(1)}, f32[192,4,128]{2,0,1:T(8,128)S(1)}) fusion(bf16[4,128,3200]{2,1,0:T(8,128)(2,1)} %bitcast.131, bf16[192,3200]{1,0:T(8,128)(2,1)} %all-gather.5.cloned.1.call-done), kind=kOutput, calls=%fused_computation.60 | convolution fusion | flops 629341440 | bytes 4901888 | tf_op jit(solution)/shard_map/dot_general | solution.py:39
  35.8 28.3 %all_gather.24 = bf16[768,512]{1,0:T(8,128)(2,1)} all-gather(bf16[192,512]{1,0:T(8,128)(2,1)S(1)} %copy_bitcast_fusion.1), channel_id=1, replica_groups=mesh['ctx'=4,'section'=2,'mp'=4] {'ctx'}, dimensions={0}, use_global_device_ids=true | all-gather | bytes 983040 | tf_op jit(solution)/shard_map/all_gather | solution.py:57
  64.1 2.3 copy.18
  66.4 3.8 %multiply_reduce_fusion.2 = (f32[192,4]{0,1:T(4,128)S(1)}, f32[192,4,128]{2,0,1:T(8,128)S(1)}) fusion(bf16[4,128,3200]{2,1,0:T(8,128)(2,1)} %bitcast.133, bf16[192,3200]{1,0:T(8,128)(2,1)} %all-gather.5.cloned.1.call-done), kind=kOutput, calls=%fused_computation.58 | convolution fusion | flops 629341440 | bytes 4901888 | tf_op jit(solution)/shard_map/dot_general | solution.py:38
  71.1 30.4 %all_gather.23 = bf16[768,512]{1,0:T(8,128)(2,1)S(1)} all-gather(bf16[192,512]{1,0:T(8,128)(2,1)S(1)} %fusion.22), channel_id=1, replica_groups=mesh['ctx'=4,'section'=2,'mp'=4] {'ctx'}, dimensions={0}, use_global_device_ids=true | all-gather | bytes 983040 | tf_op jit(solution)/shard_map/all_gather | solution.py:73
  102.7 16.9 %all-gather.9.cloned.1.call-done = bf16[1,512,3200]{1,2,0:T(8,128)(2,1)} async-done(((bf16[1,512,800]{1,2,0:T(8,128)(2,1)}), bf16[1,512,3200]{1,2,0:T(8,128)(2,1)}) %all-gather.9.cloned.1.call-update) | async-done | bytes 3276816 | tf_op jit(solution)/shard_map/all_gather | solution.py:83
  119.7 4.6 %fusion.2 = f32[192,3200]{1,0:T(8,128)} fusion(bf16[1,512,3200]{1,2,0:T(8,128)(2,1)} %all-gather.9.cloned.1.call-done, bf16[4,24,8,128]{3,2,1,0:T(8,128)(2,1)S(1)} %fusion.28), kind=kOutput, calls=%fused_computation.2 | convolution fusion | flops 629145600 | bytes 5931008 | tf_op jit(solution)/shard_map/dot_general | solution.py:81
  124.3 32.9 %reduce-scatter.3.cloned.1.call-done = f32[48,3200]{1,0:T(8,128)} async-done(((f32[192,3200]{1,0:T(8,128)}), f32[48,3200]{1,0:T(8,128)}) %reduce-scatter.3.cloned.1.call-update) | async-done | bytes 614416 | tf_op jit(solution)/shard_map/reduce_scatter | solution.py:86
  158.4 3.4 %collective-permute-start = (bf16[48,3200]{1,0:T(8,128)(2,1)S(1)}, bf16[48,3200]{1,0:T(8,128)(2,1)S(1)}, u32[]{:S(2)}, u32[]{:S(2)}) collective-permute-start(bf16[48,3200]{1,0:T(8,128)(2,1)S(1)} %fusion.37), channel_id=1, source_target_pairs={{0,4},{1,5},{2,6},{3,7},{8,12},{9,13},{10,14},{11,15},{16,20},{17,... | collective-permute-start | bytes 921608 | tf_op jit(solution)/shard_map/ppermute | solution.py:13
  161.8 6.5 %collective-permute-done = bf16[48,3200]{1,0:T(8,128)(2,1)S(1)} collective-permute-done((bf16[48,3200]{1,0:T(8,128)(2,1)S(1)}, bf16[48,3200]{1,0:T(8,128)(2,1)S(1)}, u32[]{:S(2)}, u32[]{:S(2)}) %collective-permute-start) | collective-permute-done | bytes 307232 | tf_op jit(solution)/shard_map/ppermute | solution.py:13
  171.1 18.8 %all-gather.7.cloned.1.call-done = bf16[192,3200]{1,0:T(8,128)(2,1)} async-done(((bf16[48,3200]{1,0:T(8,128)(2,1)}), bf16[192,3200]{1,0:T(8,128)(2,1)}) %all-gather.7.cloned.1.call-update) | async-done | bytes 1228816 | tf_op jit(solution)/shard_map/all_gather | solution.py:36
  190.0 4.4 %multiply_reduce_fusion = (f32[192,4]{0,1:T(4,128)S(1)}, f32[192,4,128]{2,0,1:T(8,128)}) fusion(bf16[4,128,3200]{2,1,0:T(8,128)(2,1)} %bitcast.134, bf16[192,3200]{1,0:T(8,128)(2,1)} %all-gather.7.cloned.1.call-done), kind=kOutput, calls=%fused_computation.54 | convolution fusion | flops 629341440 | bytes 4901888 | tf_op jit(solution)/shard_map/dot_general | solution.py:38
  196.0 19.9 %all_gather.28 = bf16[768,512]{1,0:T(8,128)(2,1)} all-gather(bf16[192,512]{1,0:T(8,128)(2,1)S(1)} %copy_bitcast_fusion), channel_id=1, replica_groups=mesh['ctx'=4,'section'=2,'mp'=4] {'ctx'}, dimensions={0}, use_global_device_ids=true | all-gather | bytes 983040 | tf_op jit(solution)/shard_map/all_gather | solution.py:57
  216.0 2.3 copy.25
  218.3 2.2 fusion.25
  220.5 18.2 %all_gather.27 = bf16[768,512]{1,0:T(8,128)(2,1)S(1)} all-gather(bf16[192,512]{1,0:T(8,128)(2,1)S(1)} %fusion.25), channel_id=1, replica_groups=mesh['ctx'=4,'section'=2,'mp'=4] {'ctx'}, dimensions={0}, use_global_device_ids=true | all-gather | bytes 983040 | tf_op jit(solution)/shard_map/all_gather | solution.py:73
  241.3 2.7 fusion
  244.0 32.5 %reduce-scatter.5.cloned.1.call-done = f32[48,3200]{1,0:T(8,128)} async-done(((f32[192,3200]{1,0:T(8,128)}), f32[48,3200]{1,0:T(8,128)}) %reduce-scatter.5.cloned.1.call-update) | async-done | bytes 614416 | tf_op jit(solution)/shard_map/reduce_scatter | solution.py:86
  277.7 1.9 maximum_bitcast_fusion
  (53 shorter events, 13.3 us)
Async XLA Ops:
  6.5 63.7 %copy-start = (bf16[1,3200,512]{2,1,0:T(8,128)(2,1)S(1)}, bf16[1,3200,512]{2,1,0:T(8,128)(2,1)}, u32[]{:S(2)}) copy-start(bf16[1,3200,512]{2,1,0:T(8,128)(2,1)} %param.16) | copy-start | bytes 9830404
  6.5 25.4 %all-gather.5.cloned.1.call-start = ((), (), s32[]{:S(2)}) async-start(), calls=%async_computation.2 | async-start | bytes 1536000 | tf_op jit(solution)/shard_map/all_gather | solution.py:36
  11.2 108.5 %all-gather.9.cloned.1.call-start = ((), (), s32[]{:S(2)}) async-start(), calls=%async_computation.6 | async-start | bytes 4096000 | tf_op jit(solution)/shard_map/all_gather | solution.py:83
  12.0 145.2 %reduce-scatter.3.cloned.1.call-start = ((), (), s32[]{:S(2)}) async-start(), calls=%async_computation.3 | async-start | bytes 3072000 | tf_op jit(solution)/shard_map/reduce_scatter | solution.py:86
  31.9 3.7 %copy-start.8 = (f32[1,128]{1,0:T(1,128)S(1)}, f32[1,128]{1,0:T(1,128)}, u32[]{:S(2)}) copy-start(f32[1,128]{1,0:T(1,128)} %param.13) | copy-start | bytes 1540
  66.4 3.8 %copy-start.10 = (bf16[192,3200]{1,0:T(8,128)(2,1)S(1)}, bf16[192,3200]{1,0:T(8,128)(2,1)}, u32[]{:S(2)}) copy-start(bf16[192,3200]{1,0:T(8,128)(2,1)} %all-gather.5.cloned.1.call-done) | copy-start | bytes 3686404
  70.3 31.3 %copy-start.3 = (bf16[768,512]{0,1:T(8,128)(2,1)S(1)}, bf16[768,512]{0,1:T(8,128)(2,1)}, u32[]{:S(2)}) copy-start(bf16[768,512]{0,1:T(8,128)(2,1)} %copy.18) | copy-start | bytes 2359300
  70.3 31.3 %copy-start.9 = (f32[1,128]{1,0:T(1,128)S(1)}, f32[1,128]{1,0:T(1,128)}, u32[]{:S(2)}) copy-start(f32[1,128]{1,0:T(1,128)} %param.12) | copy-start | bytes 1540
  124.3 65.7 %all-gather.7.cloned.1.call-start = ((), (), s32[]{:S(2)}) async-start(), calls=%async_computation.4 | async-start | bytes 1536000 | tf_op jit(solution)/shard_map/all_gather | solution.py:36
  158.4 3.4 %copy-start.6 = (bf16[48,3200]{1,0:T(8,128)(2,1)}, bf16[48,3200]{1,0:T(8,128)(2,1)S(1)}, u32[]{:S(2)}) copy-start(bf16[48,3200]{1,0:T(8,128)(2,1)S(1)} %fusion.37) | copy-start | bytes 921604
  158.4 9.9 %collective-permute-start = (bf16[48,3200]{1,0:T(8,128)(2,1)S(1)}, bf16[48,3200]{1,0:T(8,128)(2,1)S(1)}, u32[]{:S(2)}, u32[]{:S(2)}) collective-permute-start(bf16[48,3200]{1,0:T(8,128)(2,1)S(1)} %fusion.37), channel_id=1, source_target_pairs={{0,4},{1,5},{2,6},{3,7},{8,12},{9,13},{10,14},{11,15},{16,20},{17,... | collective-permute-start | bytes 921608 | tf_op jit(solution)/shard_map/ppermute | solution.py:13
  169.5 0.7 copy-start.5
  171.1 105.4 %reduce-scatter.5.cloned.1.call-start = ((), (), s32[]{:S(2)}) async-start(), calls=%async_computation.5 | async-start | bytes 3072000 | tf_op jit(solution)/shard_map/reduce_scatter | solution.py:86
  190.0 4.4 %copy-start.2 = (bf16[512,3200]{1,0:T(8,128)(2,1)S(1)}, bf16[512,3200]{1,0:T(8,128)(2,1)}, u32[]{:S(2)}) copy-start(bf16[512,3200]{1,0:T(8,128)(2,1)} %copy.32) | copy-start | bytes 9830404
  190.0 4.4 %copy-start.11 = (bf16[192,3200]{1,0:T(8,128)(2,1)S(1)}, bf16[192,3200]{1,0:T(8,128)(2,1)}, u32[]{:S(2)}) copy-start(bf16[192,3200]{1,0:T(8,128)(2,1)} %all-gather.7.cloned.1.call-done) | copy-start | bytes 3686404
  218.3 20.4 %copy-start.4 = (bf16[768,512]{0,1:T(8,128)(2,1)S(1)}, bf16[768,512]{0,1:T(8,128)(2,1)}, u32[]{:S(2)}) copy-start(bf16[768,512]{0,1:T(8,128)(2,1)} %copy.25) | copy-start | bytes 2359300
  218.3 20.4 %copy-start.7 = (f32[192,4,128]{2,0,1:T(8,128)S(1)}, f32[192,4,128]{2,0,1:T(8,128)}, u32[]{:S(2)}) copy-start(f32[192,4,128]{2,0,1:T(8,128)} %get-tuple-element.18) | copy-start | bytes 1179652
  239.4 1.9 copy-start.1
Sparse Core Ops, SparseCore 0:
  11.3 20.5 all-gather.4
  33.5 86.1 all-gather.8
  124.4 32.7 reduce-scatter.2
  171.2 18.7 all-gather.6
  244.1 32.2 reduce-scatter.4
where the time goes:
time: 287 us; the launch traced here: 286 us
  waiting for transfers between devices  117 us (41%)
  blocking collectives  96.9 us (34%)
  matrix products  26 us (9%)
  local copies, waits for them, and re-layouts  18.2 us (6%)
  between operations  13.3 us (5%)
  other arithmetic  11.3 us (4%)
  starting transfers between devices  3.54 us (1%)
    reduce_scatter x2, waiting for transfers between devices, per_device(): lax.psum_scatter(partial_value, 'mp', scatter_dimension=0, tiled=True)  65.3 us
    all_gather x2, blocking collectives, per_device(): lax.all_gather(projected[2], 'ctx', axis=0, tiled=True)  48.6 us
    all_gather x2, blocking collectives, per_device(): key_block = lax.all_gather(projected[1], 'ctx', axis=0, tiled=True)  48.3 us
    all_gather x2, waiting for transfers between devices, per_device(): project_segment = lax.all_gather(normed, 'mp', axis=0, tiled=True)  27.3 us
    all_gather x1, waiting for transfers between devices, per_device(): lax.all_gather(o_weight[0], 'ctx', axis=1, tiled=True)  16.9 us
    dot_general x2, matrix products, per_device(): jnp.dot(project_segment, q_weight[0], preferred_element_type=jnp.float32)  8.21 us
    dot_general x2, matrix products, per_device(): jnp.dot(attended, lax.all_gather(o_weight[0], 'ctx', axis=1, tiled=True),...  7.24 us
    ppermute x1, waiting for transfers between devices, shifted(): lax.ppermute(value, axis, [(source, source + steps) for source in range(l...  6.49 us
  transfers between devices with their start and end apart: 6, of which 6 were waited for; matrix products, arithmetic and copies ran while one was open for 8% of the time, Pallas kernels for 0%

commit v1 on v0

--- a/solution.py
+++ b/solution.py
@@ -3,8 +3,26 @@
 import jax.numpy as jnp
 from jax import lax
 from jax.sharding import PartitionSpec as P
+from jax.lax import axis_index, axis_size, ppermute
 
 epsilon = 1e-06
+
+
+def change_members_all(message):
+    buffers = [message]
+    dev_n = axis_size("mp")
+    for b in tuple(range(dev_n - 1)):
+        buffers.append(
+            ppermute(
+                buffers[-1],
+                axis_name="mp",
+                perm=[(to_i, (to_i + 1) % dev_n) for to_i in range(dev_n)],
+            )
+        )
+    right_arr = jnp.roll(
+        jnp.concatenate(buffers[::-1], axis=0), (axis_index("mp") + 1) * message.shape[0], axis=0
+    )
+    return right_arr
 
 
 def shifted(value, axis, steps):
@@ -33,7 +51,7 @@
         layer_input = jnp.where(section_index == 0, patches[micro_step], incoming)
         residual = layer_input.astype(jnp.float32)
         normed = rms_scaled(residual, layer_gain).astype(jnp.bfloat16)
-        project_segment = lax.all_gather(normed, "mp", axis=0, tiled=True)
+        project_segment = change_members_all(normed)
         project_count = project_segment.shape[0]
         raw_query = jnp.dot(project_segment, q_weight[0], preferred_element_type=jnp.float32)
         raw_key = jnp.dot(project_segment, k_weight[0], preferred_element_type=jnp.float32)

time: 287 us -> 275 us (0.958)
  waiting for transfers between devices: 117 us -> 107 us
  blocking collectives: 96.9 us -> 88.1 us
  other arithmetic: 11.3 us -> 19.2 us
    ppermute x0 -> x6, waiting for transfers between devices: none -> 31.7 us  [change_members_all(): ppermute(buffers[-1], axis_name='mp', perm=[(to_i, (to_i + 1) % dev_n) fo...]
    all_gather x2 -> x0, waiting for transfers between devices: 27.3 us -> none  [per_device(): project_segment = lax.all_gather(normed, 'mp', axis=0, tiled=True)]
    all_gather x1, waiting for transfers between devices: 16.9 us -> 0.02 us  [per_device(): lax.all_gather(o_weight[0], 'ctx', axis=1, tiled=True)]
    all_gather x2, blocking collectives: 48.6 us -> 38.1 us  [per_device(): lax.all_gather(projected[2], 'ctx', axis=0, tiled=True)]
    concatenate x0 -> x2, other arithmetic: none -> 9.16 us  [change_members_all(): jnp.roll(jnp.concatenate(buffers[::-1], axis=0), (axis_index('mp') + 1) *...]
  transfers between devices with their start and end apart: 6 -> 10, of which waited for: 6 -> 8; matrix products, arithmetic and copies ran while one was open for 8% -> 12% of each run, Pallas kernels for 0% -> 0%
where the time goes in v1:
time: 275 us
  waiting for transfers between devices  107 us (39%)
  blocking collectives  88.1 us (32%)
  matrix products  23.5 us (9%)
  local copies, waits for them, and re-layouts  19.5 us (7%)
  other arithmetic  19.2 us (7%)
  between operations  13.4 us (5%)
  starting transfers between devices  3.97 us (1%)
    reduce_scatter x2, waiting for transfers between devices, per_device(): lax.psum_scatter(partial_value, 'mp', scatter_dimension=0, tiled=True)  68 us
    all_gather x2, blocking collectives, per_device(): key_block = lax.all_gather(projected[1], 'ctx', axis=0, tiled=True)  50 us
    all_gather x2, blocking collectives, per_device(): lax.all_gather(projected[2], 'ctx', axis=0, tiled=True)  38.1 us
    ppermute x6, waiting for transfers between devices, change_members_all(): ppermute(buffers[-1], axis_name='mp', perm=[(to_i, (to_i + 1) % dev_n) fo...  31.7 us
    concatenate x2, other arithmetic, change_members_all(): jnp.roll(jnp.concatenate(buffers[::-1], axis=0), (axis_index('mp') + 1) *...  9.16 us
    dot_general x2, matrix products, per_device(): jnp.dot(attended, lax.all_gather(o_weight[0], 'ctx', axis=1, tiled=True),...  7.22 us
    ppermute x1, waiting for transfers between devices, shifted(): lax.ppermute(value, axis, [(source, source + steps) for source in range(l...  6.49 us
    dot_general x2, matrix products, per_device(): jnp.dot(project_segment, q_weight[0], preferred_element_type=jnp.float32)  5.74 us
  transfers between devices with their start and end apart: 10, of which 8 were waited for; matrix products, arithmetic and copies ran while one was open for 12% of the time, Pallas kernels for 0%

profile of v1, /device:TPU:0, one launch (start us, length us, event | category | flops | bytes accessed | tf_op | source)
XLA Modules:
  0.0 274.7 jit_solution(5258328181586461680)
XLA Ops:
  7.3 2.1 fusion.48
  12.5 6.5 %collective-permute-done = bf16[48,3200]{1,0:T(8,128)(2,1)S(1)} collective-permute-done((bf16[48,3200]{1,0:T(8,128)(2,1)S(1)}, bf16[48,3200]{1,0:T(8,128)(2,1)S(1)}, u32[]{:S(2)}, u32[]{:S(2)}) %collective-permute-start) | collective-permute-done | bytes 307232 | tf_op jit(solution)/shard_map/ppermute | solution.py:16
  19.7 6.4 %collective-permute-done.1 = bf16[48,3200]{1,0:T(8,128)(2,1)} collective-permute-done((bf16[48,3200]{1,0:T(8,128)(2,1)S(1)}, bf16[48,3200]{1,0:T(8,128)(2,1)}, u32[]{:S(2)}, u32[]{:S(2)}) %collective-permute-start.1) | collective-permute-done | bytes 307232 | tf_op jit(solution)/shard_map/ppermute | solution.py:16
  26.1 5.7 %copy.32 = bf16[512,3200]{1,0:T(8,128)(2,1)} copy(bf16[512,3200]{0,1:T(8,128)(2,1)} %bitcast.129) | data formatting | bytes 6553600 | tf_op jit(solution)/shard_map/dot_general | solution.py:57
  31.8 5.7 %copy.33 = bf16[512,3200]{1,0:T(8,128)(2,1)} copy(bf16[512,3200]{0,1:T(8,128)(2,1)} %bitcast.130) | data formatting | bytes 6553600 | tf_op jit(solution)/shard_map/dot_general | solution.py:56
  37.4 4.9 %fusion.18 = bf16[192,3200]{1,0:T(8,128)(2,1)S(1)} fusion(s32[]{:T(128)S(6)} %select_n.28, bf16[48,3200]{1,0:T(8,128)(2,1)} %collective-permute-done.2, bf16[48,3200]{1,0:T(8,128)(2,1)} %collective-permute-done.1, bf16[48,3200]{1,0:T(8,128)(2,1)} %copy-done.10, bf16[48,3200]{1,0:T(8,128)(2,1)} %copy-done.9), kind=kLoop, calls=%fused_computation.40 | loop fusion | flops 9830400 | bytes 2457604 | tf_op jit(solution)/shard_map/jit(_roll_dynamic)/concatenate | solution.py:22
  42.3 3.8 %multiply_reduce_fusion.3 = (f32[192,4]{0,1:T(4,128)S(1)}, f32[192,4,128]{2,0,1:T(8,128)S(1)}) fusion(bf16[4,128,3200]{2,1,0:T(8,128)(2,1)} %bitcast.131, bf16[192,3200]{1,0:T(8,128)(2,1)S(1)} %fusion.18), kind=kOutput, calls=%fused_computation.90 | convolution fusion | flops 629341440 | bytes 4901888 | tf_op jit(solution)/shard_map/dot_general | solution.py:57
  46.3 31.2 %all_gather.17 = bf16[768,512]{1,0:T(8,128)(2,1)} all-gather(bf16[192,512]{1,0:T(8,128)(2,1)S(1)} %copy_bitcast_fusion.1), channel_id=1, replica_groups=mesh['ctx'=4,'section'=2,'mp'=4] {'ctx'}, dimensions={0}, use_global_device_ids=true | all-gather | bytes 983040 | tf_op jit(solution)/shard_map/all_gather | solution.py:75
  77.5 2.3 copy.18
  79.8 3.8 %multiply_reduce_fusion.2 = (f32[192,4]{0,1:T(4,128)S(1)}, f32[192,4,128]{2,0,1:T(8,128)S(1)}) fusion(bf16[4,128,3200]{2,1,0:T(8,128)(2,1)} %bitcast.133, bf16[192,3200]{1,0:T(8,128)(2,1)} %copy-done.6), kind=kOutput, calls=%fused_computation.88 | convolution fusion | flops 629341440 | bytes 4901888 | tf_op jit(solution)/shard_map/dot_general | solution.py:56
  84.5 20.6 %all_gather.16 = bf16[768,512]{1,0:T(8,128)(2,1)S(1)} all-gather(bf16[192,512]{1,0:T(8,128)(2,1)S(1)} %fusion.36), channel_id=1, replica_groups=mesh['ctx'=4,'section'=2,'mp'=4] {'ctx'}, dimensions={0}, use_global_device_ids=true | all-gather | bytes 983040 | tf_op jit(solution)/shard_map/all_gather | solution.py:91
  106.3 4.6 %fusion.2 = f32[192,3200]{1,0:T(8,128)} fusion(bf16[1,512,3200]{1,2,0:T(8,128)(2,1)} %all-gather.3.cloned.1.call-done, bf16[4,24,8,128]{3,2,1,0:T(8,128)(2,1)S(1)} %fusion.42), kind=kOutput, calls=%fused_computation.2 | convolution fusion | flops 629145600 | bytes 5931008 | tf_op jit(solution)/shard_map/dot_general | solution.py:99
  111.0 33.6 %reduce-scatter.3.cloned.1.call-done = f32[48,3200]{1,0:T(8,128)} async-done(((f32[192,3200]{1,0:T(8,128)}), f32[48,3200]{1,0:T(8,128)}) %reduce-scatter.3.cloned.1.call-update) | async-done | bytes 614416 | tf_op jit(solution)/shard_map/reduce_scatter | solution.py:104
  145.9 3.4 %collective-permute-start.3 = (bf16[48,3200]{1,0:T(8,128)(2,1)S(1)}, bf16[48,3200]{1,0:T(8,128)(2,1)S(1)}, u32[]{:S(2)}, u32[]{:S(2)}) collective-permute-start(bf16[48,3200]{1,0:T(8,128)(2,1)S(1)} %fusion.51), channel_id=1, source_target_pairs={{0,4},{1,5},{2,6},{3,7},{8,12},{9,13},{10,14},{11,15},{16,20},{17,... | collective-permute-start | bytes 921608 | tf_op jit(solution)/shard_map/ppermute | solution.py:31
  149.3 6.5 %collective-permute-done.3 = bf16[48,3200]{1,0:T(8,128)(2,1)S(1)} collective-permute-done((bf16[48,3200]{1,0:T(8,128)(2,1)S(1)}, bf16[48,3200]{1,0:T(8,128)(2,1)S(1)}, u32[]{:S(2)}, u32[]{:S(2)}) %collective-permute-start.3) | collective-permute-done | bytes 307232 | tf_op jit(solution)/shard_map/ppermute | solution.py:31
  157.9 6.3 %collective-permute-done.4 = bf16[48,3200]{1,0:T(8,128)(2,1)S(1)} collective-permute-done((bf16[48,3200]{1,0:T(8,128)(2,1)S(1)}, bf16[48,3200]{1,0:T(8,128)(2,1)S(1)}, u32[]{:S(2)}, u32[]{:S(2)}) %collective-permute-start.4) | collective-permute-done | bytes 307232 | tf_op jit(solution)/shard_map/ppermute | solution.py:16
  164.2 6.3 %collective-permute-done.5 = bf16[48,3200]{1,0:T(8,128)(2,1)S(1)} collective-permute-done((bf16[48,3200]{1,0:T(8,128)(2,1)S(1)}, bf16[48,3200]{1,0:T(8,128)(2,1)S(1)}, u32[]{:S(2)}, u32[]{:S(2)}) %collective-permute-start.5) | collective-permute-done | bytes 307232 | tf_op jit(solution)/shard_map/ppermute | solution.py:16
  170.5 6.3 %collective-permute-done.6 = bf16[48,3200]{1,0:T(8,128)(2,1)S(1)} collective-permute-done((bf16[48,3200]{1,0:T(8,128)(2,1)S(1)}, bf16[48,3200]{1,0:T(8,128)(2,1)S(1)}, u32[]{:S(2)}, u32[]{:S(2)}) %collective-permute-start.6) | collective-permute-done | bytes 307232 | tf_op jit(solution)/shard_map/ppermute | solution.py:16
  176.8 4.3 %fusion.11 = bf16[192,3200]{1,0:T(8,128)(2,1)S(1)} fusion(s32[]{:T(128)S(6)} %select_n.28, bf16[48,3200]{1,0:T(8,128)(2,1)S(1)} %collective-permute-done.6, bf16[48,3200]{1,0:T(8,128)(2,1)S(1)} %collective-permute-done.5, bf16[48,3200]{1,0:T(8,128)(2,1)S(1)} %collective-permute-done.4, bf16[48,3200]{1,0:T(8,128)(2,1)S(1)} %fusion.54), kind=kLoop, calls=%fused_computation.33 | loop fusion | flops 9830400 | bytes 2457604 | tf_op jit(solution)/shard_map/jit(_roll_dynamic)/concatenate | solution.py:22
  185.5 18.8 %all_gather.20 = bf16[768,512]{1,0:T(8,128)(2,1)} all-gather(bf16[192,512]{1,0:T(8,128)(2,1)S(1)} %copy_bitcast_fusion), channel_id=1, replica_groups=mesh['ctx'=4,'section'=2,'mp'=4] {'ctx'}, dimensions={0}, use_global_device_ids=true | all-gather | bytes 983040 | tf_op jit(solution)/shard_map/all_gather | solution.py:75
  204.3 2.3 copy.25
  206.6 17.5 %all_gather.19 = bf16[768,512]{1,0:T(8,128)(2,1)S(1)} all-gather(bf16[192,512]{1,0:T(8,128)(2,1)S(1)} %fusion.39), channel_id=1, replica_groups=mesh['ctx'=4,'section'=2,'mp'=4] {'ctx'}, dimensions={0}, use_global_device_ids=true | all-gather | bytes 983040 | tf_op jit(solution)/shard_map/all_gather | solution.py:91
  228.0 2.7 fusion
  230.7 34.4 %reduce-scatter.5.cloned.1.call-done = f32[48,3200]{1,0:T(8,128)} async-done(((f32[192,3200]{1,0:T(8,128)}), f32[48,3200]{1,0:T(8,128)}) %reduce-scatter.5.cloned.1.call-update) | async-done | bytes 614416 | tf_op jit(solution)/shard_map/reduce_scatter | solution.py:104
  (63 shorter events, 21.6 us)
Async XLA Ops:
  6.5 77.1 %copy-start = (bf16[1,3200,512]{2,1,0:T(8,128)(2,1)S(1)}, bf16[1,3200,512]{2,1,0:T(8,128)(2,1)}, u32[]{:S(2)}) copy-start(bf16[1,3200,512]{2,1,0:T(8,128)(2,1)} %param.18) | copy-start | bytes 9830404
  6.5 99.8 %all-gather.3.cloned.1.call-start = ((), (), s32[]{:S(2)}) async-start(), calls=%async_computation.4 | async-start | bytes 4096000 | tf_op jit(solution)/shard_map/all_gather | solution.py:101
  7.3 137.3 %reduce-scatter.3.cloned.1.call-start = ((), (), s32[]{:S(2)}) async-start(), calls=%async_computation.2 | async-start | bytes 3072000 | tf_op jit(solution)/shard_map/reduce_scatter | solution.py:104
  11.3 0.7 copy-start.9
  12.0 6.9 %collective-permute-start = (bf16[48,3200]{1,0:T(8,128)(2,1)S(1)}, bf16[48,3200]{1,0:T(8,128)(2,1)S(1)}, u32[]{:S(2)}, u32[]{:S(2)}) collective-permute-start(bf16[48,3200]{1,0:T(8,128)(2,1)S(1)} %fusion.50), channel_id=1, source_target_pairs={{0,1},{1,2},{2,3},{3,0},{4,5},{5,6},{6,7},{7,4},{8,9},{9,10},{10,1... | collective-permute-start | bytes 921608 | tf_op jit(solution)/shard_map/ppermute | solution.py:16
  19.0 0.7 copy-start.10
  19.7 6.4 %collective-permute-start.1 = (bf16[48,3200]{1,0:T(8,128)(2,1)S(1)}, bf16[48,3200]{1,0:T(8,128)(2,1)}, u32[]{:S(2)}, u32[]{:S(2)}) collective-permute-start(bf16[48,3200]{1,0:T(8,128)(2,1)S(1)} %collective-permute-done), channel_id=1, source_target_pairs={{0,1},{1,2},{2,3},{3,0},{4,5},{5,6},{6,7},{7,4},{8,9},{9,10},{10,1... | collective-permute-start | bytes 921608 | tf_op jit(solution)/shard_map/ppermute | solution.py:16
  26.1 11.3 %collective-permute-start.2 = (bf16[48,3200]{1,0:T(8,128)(2,1)}, bf16[48,3200]{1,0:T(8,128)(2,1)}, u32[]{:S(2)}, u32[]{:S(2)}) collective-permute-start(bf16[48,3200]{1,0:T(8,128)(2,1)} %collective-permute-done.1), channel_id=1, source_target_pairs={{0,1},{1,2},{2,3},{3,0},{4,5},{5,6},{6,7},{7,4},{8,9},{9,10},{10,1... | collective-permute-start | bytes 921608 | tf_op jit(solution)/shard_map/ppermute | solution.py:16
  42.3 3.8 %copy-start.6 = (bf16[192,3200]{1,0:T(8,128)(2,1)}, bf16[192,3200]{1,0:T(8,128)(2,1)S(1)}, u32[]{:S(2)}) copy-start(bf16[192,3200]{1,0:T(8,128)(2,1)S(1)} %fusion.18) | copy-start | bytes 3686404
  42.3 3.8 %copy-start.11 = (f32[1,128]{1,0:T(1,128)S(1)}, f32[1,128]{1,0:T(1,128)}, u32[]{:S(2)}) copy-start(f32[1,128]{1,0:T(1,128)} %param.15) | copy-start | bytes 1540
  79.8 3.8 %copy-start.7 = (bf16[192,3200]{1,0:T(8,128)(2,1)S(1)}, bf16[192,3200]{1,0:T(8,128)(2,1)}, u32[]{:S(2)}) copy-start(bf16[192,3200]{1,0:T(8,128)(2,1)} %copy-done.6) | copy-start | bytes 3686404
  83.6 21.4 %copy-start.4 = (bf16[768,512]{0,1:T(8,128)(2,1)S(1)}, bf16[768,512]{0,1:T(8,128)(2,1)}, u32[]{:S(2)}) copy-start(bf16[768,512]{0,1:T(8,128)(2,1)} %copy.18) | copy-start | bytes 2359300
  83.6 21.4 %copy-start.12 = (f32[1,128]{1,0:T(1,128)S(1)}, f32[1,128]{1,0:T(1,128)}, u32[]{:S(2)}) copy-start(f32[1,128]{1,0:T(1,128)} %param.14) | copy-start | bytes 1540
  110.9 154.1 %reduce-scatter.5.cloned.1.call-start = ((), (), s32[]{:S(2)}) async-start(), calls=%async_computation.3 | async-start | bytes 3072000 | tf_op jit(solution)/shard_map/reduce_scatter | solution.py:104
  144.6 36.5 %copy-start.3 = (bf16[512,3200]{1,0:T(8,128)(2,1)S(1)}, bf16[512,3200]{1,0:T(8,128)(2,1)}, u32[]{:S(2)}) copy-start(bf16[512,3200]{1,0:T(8,128)(2,1)} %copy.33) | copy-start | bytes 9830404
  145.9 3.4 %copy-start.8 = (bf16[48,3200]{1,0:T(8,128)(2,1)}, bf16[48,3200]{1,0:T(8,128)(2,1)S(1)}, u32[]{:S(2)}) copy-start(bf16[48,3200]{1,0:T(8,128)(2,1)S(1)} %fusion.51) | copy-start | bytes 921604
  145.9 9.9 %collective-permute-start.3 = (bf16[48,3200]{1,0:T(8,128)(2,1)S(1)}, bf16[48,3200]{1,0:T(8,128)(2,1)S(1)}, u32[]{:S(2)}, u32[]{:S(2)}) collective-permute-start(bf16[48,3200]{1,0:T(8,128)(2,1)S(1)} %fusion.51), channel_id=1, source_target_pairs={{0,4},{1,5},{2,6},{3,7},{8,12},{9,13},{10,14},{11,15},{16,20},{17,... | collective-permute-start | bytes 921608 | tf_op jit(solution)/shard_map/ppermute | solution.py:31
  157.0 0.7 copy-start.5
  157.9 6.3 %collective-permute-start.4 = (bf16[48,3200]{1,0:T(8,128)(2,1)S(1)}, bf16[48,3200]{1,0:T(8,128)(2,1)S(1)}, u32[]{:S(2)}, u32[]{:S(2)}) collective-permute-start(bf16[48,3200]{1,0:T(8,128)(2,1)S(1)} %fusion.54), channel_id=1, source_target_pairs={{0,1},{1,2},{2,3},{3,0},{4,5},{5,6},{6,7},{7,4},{8,9},{9,10},{10,1... | collective-permute-start | bytes 921608 | tf_op jit(solution)/shard_map/ppermute | solution.py:16
  164.2 6.3 %collective-permute-start.5 = (bf16[48,3200]{1,0:T(8,128)(2,1)S(1)}, bf16[48,3200]{1,0:T(8,128)(2,1)S(1)}, u32[]{:S(2)}, u32[]{:S(2)}) collective-permute-start(bf16[48,3200]{1,0:T(8,128)(2,1)S(1)} %collective-permute-done.4), channel_id=1, source_target_pairs={{0,1},{1,2},{2,3},{3,0},{4,5},{5,6},{6,7},{7,4},{8,9},{9,10},{10,1... | collective-permute-start | bytes 921608 | tf_op jit(solution)/shard_map/ppermute | solution.py:16
  170.5 6.3 %collective-permute-start.6 = (bf16[48,3200]{1,0:T(8,128)(2,1)S(1)}, bf16[48,3200]{1,0:T(8,128)(2,1)S(1)}, u32[]{:S(2)}, u32[]{:S(2)}) collective-permute-start(bf16[48,3200]{1,0:T(8,128)(2,1)S(1)} %collective-permute-done.5), channel_id=1, source_target_pairs={{0,1},{1,2},{2,3},{3,0},{4,5},{5,6},{6,7},{7,4},{8,9},{9,10},{10,1... | collective-permute-start | bytes 921608 | tf_op jit(solution)/shard_map/ppermute | solution.py:16
  181.1 2.0 copy-start.2
  226.1 1.9 copy-start.1
Sparse Core Ops, SparseCore 0:
  8.9 80.8 all-gather.2
  111.0 33.4 reduce-scatter.2
  230.8 34.2 reduce-scatter.4
